TPU v7x, 32 devices: a whole 2x2x4 slice. The times are simulated.
32 devices in a mesh: row: 4 (over z), col: 8 (over y, x, core).
Axes of the slice: x: 2, y: 2, z: 4, core: 2. Of those that a mesh axis runs over, the one named last changes fastest.
Arguments:
- factor_panel: bfloat16 [2, 1536, 24576], P(None, 'row', 'col'), may hold values from -0.0390625 to 0.0390625
- solved_trail: bfloat16 [24576, 384], P('col'), may hold values from -6 to 6
- right_sides: bfloat16 [2, 1536, 384], P(None, 'row'), may hold values from -6 to 6
- diag_inverse: bfloat16 [2, 1536, 1536], P(None, 'row'), may hold values from -1 to 1.5, as said below
- coupling: bfloat16 [1536, 1536], P('row'), may hold values from -0.15625 to 0.15625
Outputs:
- solution: bfloat16 [2, 1536, 384], P(None, 'row')
Inputs may be any that keep to these rules, and one draw needn't show every extreme that they name: Each diag_inverse[b] is upper triangular with a diagonal between 0.6 and 1.4.
All inputs are finite; a program needn't handle non-finite values.
Results may differ from a plain program's by a relative error of at most 0.0057.
Values may be sent and summed in bfloat16 or wider, within the bound.
A program may use at most 64 MiB of HBM per device.

v0:
```python
import jax
import jax.numpy as jnp
from jax import lax
from jax.sharding import PartitionSpec as P


def substitute(totals, rights, diag_inverse, coupling):
    next_res = (rights[1].astype(jnp.float32) - totals[1]).astype(jnp.bfloat16)
    columns = diag_inverse[1]
    next_sol = jnp.dot(
        columns,
        lax.all_gather(next_res, "row", axis=0, tiled=True),
        preferred_element_type=jnp.float32,
    ).astype(jnp.bfloat16)
    columns = coupling
    carried = jnp.dot(
        columns,
        lax.all_gather(next_sol, "row", axis=0, tiled=True),
        preferred_element_type=jnp.float32,
    )
    first_res = (rights[0].astype(jnp.float32) - totals[0] - carried).astype(jnp.bfloat16)
    columns = diag_inverse[0]
    first_sol = jnp.dot(
        columns,
        lax.all_gather(first_res, "row", axis=0, tiled=True),
        preferred_element_type=jnp.float32,
    ).astype(jnp.bfloat16)
    return jnp.stack([first_sol, next_sol])


def reduce_updates(factor_panel, trail_part):
    partial_value = jnp.einsum(
        "bik,kf->bif", factor_panel, trail_part, preferred_element_type=jnp.float32
    )
    return lax.psum(partial_value, "col")


def shards(factor_panel, solved_trail, right_sides, diag_inverse, coupling):
    totals = reduce_updates(factor_panel, solved_trail)
    return substitute(totals, right_sides, diag_inverse, coupling)


def solution(mesh):
    in_specs = (
        P(None, "row", "col"),
        P("col", None),
        P(None, "row", None),
        P(None, "row", None),
        P("row", None),
    )
    out_specs = P(None, "row", None)
    return jax.shard_map(shards, mesh=mesh, in_specs=in_specs, out_specs=out_specs, check_vma=False)
```

profile of v0, /device:TPU:0, one launch (start us, length us, event | category | flops | bytes accessed | tf_op | source)
XLA Modules:
  0.0 181.6 jit_solution(15904181698284857279)
XLA Ops:
  6.5 0.0 copy-start
  6.5 0.0 all-reduce.2.cloned.1.call-start
  6.5 1.7 copy-done
  8.2 5.9 %fusion = f32[2,384,384]{2,1,0:T(8,128)} fusion(bf16[2,384,3072]{2,1,0:T(8,128)(2,1)} %param.5, bf16[3072,384]{1,0:T(8,128)(2,1)S(1)} %copy-done), kind=kOutput, calls=%fused_computation | convolution fusion | flops 1811939328 | bytes 8257536 | tf_op jit(solution)/shard_map/bik,kf->bif/dot_general | solution.py:32
  14.2 0.0 all-reduce.2.cloned.1.call-update
  14.2 0.0 all-gather.9.cloned.1.call-start
  14.2 60.0 %all-reduce.2.cloned.1.call-done = f32[2,384,384]{2,1,0:T(8,128)} async-done(((f32[2,384,384]{2,1,0:T(8,128)}), f32[2,384,384]{2,1,0:T(8,128)}) %all-reduce.2.cloned.1.call-update) | async-done | bytes 1179664 | tf_op jit(solution)/shard_map/psum | solution.py:35
  74.3 0.0 copy-done.3
  74.3 1.8 %fusion.12 = bf16[1,384,384]{2,1,0:T(8,128)(2,1)} fusion(f32[2,384,384]{2,1,0:T(8,128)} %all-reduce.2.cloned.1.call-done, bf16[2,384,384]{2,1,0:T(8,128)(2,1)S(1)} %copy-done.3), kind=kLoop, calls=%fused_computation.14 | loop fusion | flops 442368 | bytes 1179648 | tf_op jit(solution)/shard_map/convert_element_type | solution.py:8
  76.1 0.0 all-gather.9.cloned.1.call-update
  76.1 0.0 all-gather.5.cloned.1.call-start
  76.2 29.6 %all-gather.9.cloned.1.call-done = bf16[1,1536,384]{2,1,0:T(8,128)(2,1)} async-done(((bf16[1,384,384]{2,1,0:T(8,128)(2,1)}), bf16[1,1536,384]{2,1,0:T(8,128)(2,1)}) %all-gather.9.cloned.1.call-update) | async-done | bytes 1179664 | tf_op jit(solution)/shard_map/all_gather | solution.py:12
  105.8 3.2 %convolution_convert_fusion.1 = bf16[384,384]{1,0:T(8,128)(2,1)} fusion(bf16[1,1536,384]{2,1,0:T(8,128)(2,1)} %all-gather.9.cloned.1.call-done, bf16[2,384,1536]{2,1,0:T(8,128)(2,1)} %param.8), kind=kOutput, calls=%fused_computation.5 | convolution fusion | flops 453132288 | bytes 2654208 | tf_op jit(solution)/shard_map/dot_general | solution.py:10
  108.9 0.0 all-gather.5.cloned.1.call-update
  109.0 0.0 all-gather.7.cloned.1.call-start
  109.0 29.5 %all-gather.5.cloned.1.call-done = bf16[1536,384]{0,1:T(8,128)(2,1)} async-done(((bf16[384,384]{0,1:T(8,128)(2,1)}), bf16[1536,384]{0,1:T(8,128)(2,1)}) %all-gather.5.cloned.1.call-update) | async-done | bytes 1179664 | tf_op jit(solution)/shard_map/all_gather | solution.py:18
  138.5 0.0 copy-done.2
  138.5 3.2 %fusion.3 = bf16[384,384]{1,0:T(8,128)(2,1)} fusion(bf16[1536,384]{0,1:T(8,128)(2,1)} %all-gather.5.cloned.1.call-done, bf16[384,1536]{1,0:T(8,128)(2,1)} %param.9, f32[2,384,384]{2,1,0:T(8,128)S(1)} %copy-done.2, bf16[2,384,384]{2,1,0:T(8,128)(2,1)} %param.7), kind=kOutput, calls=%fused_computation.6 | convolution fusion | flops 453574656 | bytes 3538944 | tf_op jit(solution)/shard_map/dot_general | solution.py:16
  141.7 0.0 all-gather.7.cloned.1.call-update
  141.7 0.0 copy-start.1
  141.7 29.7 %all-gather.7.cloned.1.call-done = bf16[1536,384]{1,0:T(8,128)(2,1)} async-done(((bf16[384,384]{1,0:T(8,128)(2,1)}), bf16[1536,384]{1,0:T(8,128)(2,1)}) %all-gather.7.cloned.1.call-update) | async-done | bytes 1179664 | tf_op jit(solution)/shard_map/all_gather | solution.py:25
  171.5 2.4 %fusion.9 = bf16[1,384,384]{1,2,0:T(8,128)(2,1)S(1)} fusion(bf16[1536,384]{1,0:T(8,128)(2,1)} %all-gather.7.cloned.1.call-done, bf16[2,384,1536]{2,1,0:T(8,128)(2,1)} %param.8), kind=kOutput, calls=%fused_computation.12 | convolution fusion | flops 453132288 | bytes 2654208 | tf_op jit(solution)/shard_map/dot_general | solution.py:23
  173.9 0.1 pad_maximum_fusion
  174.0 1.1 copy.6
  (3 shorter events, 0.0 us)
Async XLA Ops:
  6.5 1.7 copy-start
  6.5 67.7 %all-reduce.2.cloned.1.call-start = ((), (), s32[]{:S(2)}) async-start(), calls=%async_computation | async-start | bytes 2359296 | tf_op jit(solution)/shard_map/psum | solution.py:35
  14.1 60.1 %copy-start.3 = (bf16[2,384,384]{2,1,0:T(8,128)(2,1)S(1)}, bf16[2,384,384]{2,1,0:T(8,128)(2,1)}, u32[]{:S(2)}) copy-start(bf16[2,384,384]{2,1,0:T(8,128)(2,1)} %param.7) | copy-start | bytes 1769476
  14.2 91.6 %all-gather.9.cloned.1.call-start = ((), (), s32[]{:S(2)}) async-start(), calls=%async_computation.3 | async-start | bytes 1474560 | tf_op jit(solution)/shard_map/all_gather | solution.py:12
  76.1 62.4 %copy-start.2 = (f32[2,384,384]{2,1,0:T(8,128)S(1)}, f32[2,384,384]{2,1,0:T(8,128)}, u32[]{:S(2)}) copy-start(f32[2,384,384]{2,1,0:T(8,128)} %all-reduce.2.cloned.1.call-done) | copy-start | bytes 3538948
  76.1 62.4 %all-gather.5.cloned.1.call-start = ((), (), s32[]{:S(2)}) async-start(), calls=%async_computation.1 | async-start | bytes 1474560 | tf_op jit(solution)/shard_map/all_gather | solution.py:18
  109.0 62.5 %all-gather.7.cloned.1.call-start = ((), (), s32[]{:S(2)}) async-start(), calls=%async_computation.2 | async-start | bytes 1474560 | tf_op jit(solution)/shard_map/all_gather | solution.py:25
  141.7 32.2 %copy-start.1 = (bf16[384,384]{1,0:T(8,128)(2,1)S(1)}, bf16[384,384]{1,0:T(8,128)(2,1)}, u32[]{:S(2)}) copy-start(bf16[384,384]{1,0:T(8,128)(2,1)} %convolution_convert_fusion.1) | copy-start | bytes 884740
Sparse Core Ops, SparseCore 0:
  14.3 59.9 all-reduce.1
  76.3 29.4 all-gather.8
  109.1 29.3 all-gather.4
  141.8 29.5 all-gather.6
where the time goes:
time: 182 us
  waiting for transfers between devices  149 us (82%)
  matrix products  14.7 us (8%)
  between operations  13.2 us (7%)
  local copies, waits for them, and re-layouts  2.74 us (2%)
  other arithmetic  1.9 us (1%)
    psum x1, waiting for transfers between devices, reduce_updates(): return lax.psum(partial_value, 'col')  60 us
    all_gather x1, waiting for transfers between devices, substitute(): lax.all_gather(first_res, 'row', axis=0, tiled=True)  29.7 us
    all_gather x1, waiting for transfers between devices, substitute(): lax.all_gather(next_res, 'row', axis=0, tiled=True)  29.6 us
    all_gather x1, waiting for transfers between devices, substitute(): lax.all_gather(next_sol, 'row', axis=0, tiled=True)  29.5 us
    dot_general x1, matrix products, reduce_updates(): jnp.einsum('bik,kf->bif', factor_panel, trail_part, preferred_element_typ...  5.95 us
  transfers between devices with their start and end apart: 4, of which 4 were waited for; matrix products, arithmetic and copies ran while one was open for 0% of the time, Pallas kernels for 0%

commit v1 on v0

v1 whole, which is shorter than its diff:
```python
import functools

import jax
import jax.numpy as jnp
from jax import lax
from jax.experimental import pallas as pl
from jax.experimental.pallas import tpu as pltpu
from jax.sharding import PartitionSpec as P

F32 = jnp.float32
BF16 = jnp.bfloat16
MESH = pl.DeviceIdType.MESH


def substitute(totals, rights, diag_inverse, coupling):
    next_res = (rights[1].astype(F32) - totals[1]).astype(BF16)
    next_all = lax.all_gather(next_res, "row", axis=0, tiled=True)
    next_sol = jnp.dot(diag_inverse[1], next_all, preferred_element_type=F32).astype(BF16)
    sol_all = lax.all_gather(next_sol, "row", axis=0, tiled=True)
    carried = jnp.dot(coupling, sol_all, preferred_element_type=F32)
    first_res = (rights[0].astype(F32) - totals[0] - carried).astype(BF16)
    first_all = lax.all_gather(first_res, "row", axis=0, tiled=True)
    first_sol = jnp.dot(diag_inverse[0], first_all, preferred_element_type=F32).astype(BF16)
    return jnp.stack([first_sol, next_sol])


def plain_shards(factor_panel, solved_trail, right_sides, diag_inverse, coupling):
    partial_value = jnp.einsum(
        "bik,kf->bif", factor_panel, solved_trail, preferred_element_type=F32
    )
    totals = lax.psum(partial_value, "col")
    return substitute(totals, right_sides, diag_inverse, coupling)


def dot_t(a, b):
    return lax.dot_general(a, b, (((1,), (1,)), ((), ())), preferred_element_type=F32)


def kernel(
    R, C, nk,
    panel, trail, right, diag, coup, out,
    pbuf, tbuf, hbuf, mbuf, acc, acc_t, h_t, sbuf, gbuf, zbuf, zacc, fbuf,
    psem, tsem, hsem, msem, lsem, gsend, grecv, zsend, zrecv, fsend, frecv,
):
    r = lax.axis_index("row")
    c = lax.axis_index("col")
    m, frames = hbuf.shape[1], hbuf.shape[2]
    kc = tbuf.shape[1]
    fs = frames // C

    def flip(d):
        total = 0
        bit = 1
        while bit < C:
            mine = (c // bit) % 2
            total = total + (((mine + 1) % 2) if d & bit else mine) * bit
            bit *= 2
        return total

    peers = [flip(d) for d in range(1, C)][::-1]

    def panel_copy(b, i):
        return pltpu.make_async_copy(
            panel.at[b, :, pl.ds(i * kc, kc)], pbuf.at[b, i], psem.at[b, i]
        )

    def trail_copy(i):
        return pltpu.make_async_copy(trail.at[pl.ds(i * kc, kc), :], tbuf.at[i], tsem.at[i])

    def mat_copy(b, j):
        src = coup.at[:, pl.ds(j * m, m)] if b == 2 else diag.at[b, :, pl.ds(j * m, m)]
        return pltpu.make_async_copy(src, mbuf.at[b, j], msem.at[b, j])

    right_copy = pltpu.make_async_copy(right, hbuf, hsem)
    for i in range(nk):
        trail_copy(i).start()
        panel_copy(1, i).start()
    for i in range(nk):
        panel_copy(0, i).start()
    right_copy.start()
    for b in (1, 2, 0):
        for j in range(R):
            mat_copy(b, j).start()

    barrier = pltpu.get_barrier_semaphore()
    for p in peers:
        pl.semaphore_signal(barrier, inc=1, device_id=(r, p), device_id_type=MESH)
    for d in range(1, R):
        pl.semaphore_signal(
            barrier, inc=1, device_id=(lax.rem(r + d, R), c), device_id_type=MESH
        )

    def part_send(b, n):
        p = peers[n]
        return pltpu.make_async_remote_copy(
            src_ref=sbuf.at[b, p], dst_ref=gbuf.at[b, c],
            send_sem=gsend.at[b, n], recv_sem=grecv.at[b, c],
            device_id=(r, p), device_id_type=MESH,
        )

    def part_recv(b, n):
        p = peers[n]
        return pltpu.make_async_remote_copy(
            src_ref=sbuf.at[b, p], dst_ref=gbuf.at[b, p],
            send_sem=gsend.at[b, n], recv_sem=grecv.at[b, p],
            device_id=(r, p), device_id_type=MESH,
        )

    def partials(b):
        for i in range(nk):
            if b == 1:
                trail_copy(i).wait()
            panel_copy(b, i).wait()
            term = jnp.dot(pbuf[b, i], tbuf[i], preferred_element_type=F32)
            if i == 0:
                acc[...] = term
            else:
                acc[...] += term
        turned = acc[...].T.reshape(C, fs, m)
        sbuf[b] = turned.astype(BF16)
        acc_t[b] = turned

    partials(1)
    pl.semaphore_wait(barrier, C - 1 + R - 1)
    for n in range(C - 1):
        part_send(1, n).start()
    partials(0)
    for n in range(C - 1):
        part_send(0, n).start()
    right_copy.wait()
    for b in (1, 0):
        h_t[b] = hbuf[b].astype(F32).T.reshape(C, fs, m)
    for b in (1, 2, 0):
        for j in range(R):
            mat_copy(b, j).wait()

    def residual(b):
        total = acc_t[b, c]
        for n in reversed(range(C - 1)):
            part_recv(b, n).wait_recv()
            total = total + gbuf[b, peers[n]].astype(F32)
        return h_t[b, c] - total

    def row_send(phase, j):
        return pltpu.make_async_remote_copy(
            src_ref=zbuf.at[phase, r], dst_ref=zbuf.at[phase, r],
            send_sem=zsend.at[phase, j], recv_sem=zrecv.at[phase, r],
            device_id=(j, c), device_id_type=MESH,
        )

    def row_recv(phase, j):
        return pltpu.make_async_remote_copy(
            src_ref=zbuf.at[phase, j], dst_ref=zbuf.at[phase, j],
            send_sem=zsend.at[phase, j], recv_sem=zrecv.at[phase, j],
            device_id=(j, c), device_id_type=MESH,
        )

    def triangle(phase, b, value):
        zbuf[phase, r] = value
        for d in reversed(range(1, R)):
            @pl.when(r - d >= 0)
            def _():
                row_send(phase, r - d).start()
        zacc[...] = dot_t(zbuf[phase, r], mbuf[b, r])
        for d in range(1, R):
            @pl.when(r + d < R)
            def _():
                row_recv(phase, r + d).wait_recv()
                zacc[...] += dot_t(zbuf[phase, r + d], mbuf[b, r + d])
        return zacc[...].astype(BF16)

    def sol_send(b, n):
        p = peers[n]
        return pltpu.make_async_remote_copy(
            src_ref=fbuf.at[b], dst_ref=out.at[b, c],
            send_sem=fsend.at[b, n], recv_sem=frecv.at[b, c],
            device_id=(r, p), device_id_type=MESH,
        )

    def sol_recv(b, n):
        p = peers[n]
        return pltpu.make_async_remote_copy(
            src_ref=fbuf.at[b], dst_ref=out.at[b, p],
            send_sem=fsend.at[b, n], recv_sem=frecv.at[b, p],
            device_id=(r, p), device_id_type=MESH,
        )

    def own_copy(b):
        return pltpu.make_async_copy(fbuf.at[b], out.at[b, c], lsem.at[b])

    next_sol = triangle(0, 1, residual(1).astype(BF16))

    zbuf[1, r] = next_sol
    for d in reversed(range(1, R)):
        @pl.when(r - d >= 0)
        def _():
            row_send(1, r - d).start()

        @pl.when(r + d < R)
        def _():
            row_send(1, r + d).start()
    fbuf[1] = next_sol
    for n in range(C - 1):
        sol_send(1, n).start()
    own_copy(1).start()

    zacc[...] = residual(0)
    for j in reversed(range(R)):
        @pl.when(r != j)
        def _():
            row_recv(1, j).wait_recv()
        zacc[...] -= dot_t(zbuf[1, j], mbuf[2, j])

    first_sol = triangle(2, 0, zacc[...].astype(BF16))
    fbuf[0] = first_sol
    for n in range(C - 1):
        sol_send(0, n).start()
    own_copy(0).start()

    for b in (1, 0):
        own_copy(b).wait()
        for n in range(C - 1):
            sol_recv(b, n).wait_recv()
    for b in (1, 0):
        for n in range(C - 1):
            part_send(b, n).wait_send()
            sol_send(b, n).wait_send()
    for phase in range(3):
        for d in range(1, R):
            @pl.when(r - d >= 0)
            def _():
                row_send(phase, r - d).wait_send()
            if phase == 1:
                @pl.when(r + d < R)
                def _():
                    row_send(phase, r + d).wait_send()


def fused_shards(R, C, factor_panel, solved_trail, right_sides, diag_inverse, coupling):
    _, m, k = factor_panel.shape
    frames = solved_trail.shape[1]
    fs = frames // C
    nk = 4
    kc = k // nk
    any_spec = pl.BlockSpec(memory_space=pl.ANY)
    DMA = pltpu.SemaphoreType.DMA
    out = pl.pallas_call(
        functools.partial(kernel, R, C, nk),
        out_shape=jax.ShapeDtypeStruct((2, C, fs, m), BF16),
        in_specs=[any_spec] * 5,
        out_specs=any_spec,
        scratch_shapes=[
            pltpu.VMEM((2, nk, m, kc), BF16),
            pltpu.VMEM((nk, kc, frames), BF16),
            pltpu.VMEM((2, m, frames), BF16),
            pltpu.VMEM((3, R, m, m), BF16),
            pltpu.VMEM((m, frames), F32),
            pltpu.VMEM((2, C, fs, m), F32),
            pltpu.VMEM((2, C, fs, m), F32),
            pltpu.VMEM((2, C, fs, m), BF16),
            pltpu.VMEM((2, C, fs, m), BF16),
            pltpu.VMEM((3, R, fs, m), BF16),
            pltpu.VMEM((fs, m), F32),
            pltpu.VMEM((2, fs, m), BF16),
            DMA((2, nk)),
            DMA((nk,)),
            DMA,
            DMA((3, R)),
            DMA((2,)),
            DMA((2, C - 1)),
            DMA((2, C)),
            DMA((3, R)),
            DMA((3, R)),
            DMA((2, C - 1)),
            DMA((2, C)),
        ],
        compiler_params=pltpu.CompilerParams(collective_id=0, has_side_effects=True),
    )(factor_panel, solved_trail, right_sides, diag_inverse, coupling)
    return jnp.swapaxes(out.reshape(2, frames, m), 1, 2)


def solution(mesh):
    R, C = mesh.shape["row"], mesh.shape["col"]

    def shards(factor_panel, solved_trail, right_sides, diag_inverse, coupling):
        _, m, k = factor_panel.shape
        frames = solved_trail.shape[1]
        fits = (
            C & (C - 1) == 0 and frames % (16 * C) == 0 and m % 128 == 0
            and frames % 128 == 0 and k % 512 == 0
        )
        args = (factor_panel, solved_trail, right_sides, diag_inverse, coupling)
        return fused_shards(R, C, *args) if fits else plain_shards(*args)

    in_specs = (
        P(None, "row", "col"),
        P("col", None),
        P(None, "row", None),
        P(None, "row", None),
        P("row", None),
    )
    out_specs = P(None, "row", None)
    return jax.shard_map(shards, mesh=mesh, in_specs=in_specs, out_specs=out_specs, check_vma=False)
```

time: 182 us -> 35.7 us (0.20)
  waiting for transfers between devices: 149 us -> 0 us
  Pallas kernels: 0 us -> 33.4 us
  matrix products: 14.7 us -> 0 us
  between operations: 13.2 us -> 0.01 us
  other arithmetic: 1.9 us -> 0 us
    all_gather x3 -> x0, waiting for transfers between devices: 88.8 us -> none  [the longest x1 29.7 us: substitute(): lax.all_gather(first_res, 'row', axis=0, tiled=True)]
    psum x1 -> x0, waiting for transfers between devices: 60 us -> none  [reduce_updates(): return lax.psum(partial_value, 'col')]
    pallas_call x0 -> x1, Pallas kernels: none -> 33.4 us  [fused_shards(): pl.pallas_call(functools.partial(kernel, R, C, nk), out_shape=jax.ShapeDt...]
    dot_general x4 -> x0, matrix products: 14.7 us -> none  [the longest x1 5.95 us: reduce_updates(): jnp.einsum('bik,kf->bif', factor_panel, trail_part, preferred_element_typ...]
    reshape x0 -> x1, local copies, waits for them, and re-layouts: none -> 2.12 us  [fused_shards(): return jnp.swapaxes(out.reshape(2, frames, m), 1, 2)]
    convert_element_type x1 -> x0, other arithmetic: 1.84 us -> none  [substitute(): next_res = (rights[1].astype(jnp.float32) - totals[1]).astype(jnp.bfloat16)]
  transfers between devices with their start and end apart: 4 -> 0, of which waited for: 4 -> 0; matrix products, arithmetic and copies ran while one was open for 0% -> 0% of each run, Pallas kernels for 0% -> 0%
where the time goes in v1:
time: 35.7 us; the launch traced here: 35.5 us
  Pallas kernels  33.4 us (94%)
  local copies, waits for them, and re-layouts  2.12 us (6%)
    pallas_call x1, Pallas kernels, fused_shards(): pl.pallas_call(functools.partial(kernel, R, C, nk), out_shape=jax.ShapeDt...  33.4 us
    reshape x1, local copies, waits for them, and re-layouts, fused_shards(): return jnp.swapaxes(out.reshape(2, frames, m), 1, 2)  2.12 us

profile of v1, /device:TPU:0, one launch (start us, length us, event | category | flops | bytes accessed | tf_op | source)
XLA Modules:
  0.0 35.5 jit_solution(12062721255775932306)
XLA Ops:
  0.0 33.4 %shard_map.55 = bf16[2,8,48,384]{3,2,1,0:T(8,128)(2,1)} custom-call(bf16[2,384,3072]{2,1,0:T(8,128)(2,1)} %panel.1, bf16[3072,384]{1,0:T(8,128)(2,1)} %trail.1, bf16[2,384,384]{2,1,0:T(8,128)(2,1)} %right.1, bf16[2,384,1536]{2,1,0:T(8,128)(2,1)} %diag.1, bf16[384,1536]{1,0:T(8,128)(2,1)} %coup.1), custom_call_target="tpu_custom_call" | custom-call | tf_op jit(solution)/shard_map/pallas_call | solution.py:247
  33.4 2.1 %copy.6 = bf16[2,384,384]{1,2,0:T(8,128)(2,1)} copy(bf16[2,384,384]{2,1,0:T(8,128)(2,1)} %bitcast.2) | data formatting | bytes 1179648 | tf_op jit(solution)/shard_map/reshape | solution.py:279

commit v2 on v1

--- a/solution.py
+++ b/solution.py
@@ -39,8 +39,8 @@
 def kernel(
     R, C, nk,
     panel, trail, right, diag, coup, out,
-    pbuf, tbuf, hbuf, mbuf, acc, acc_t, h_t, sbuf, gbuf, zbuf, zacc, fbuf,
-    psem, tsem, hsem, msem, lsem, gsend, grecv, zsend, zrecv, fsend, frecv,
+    pbuf, tbuf, hbuf, mbuf, acc, acc_t, h_t, sbuf, gbuf, zbuf, zacc, fbuf, xbuf, ybuf,
+    psem, tsem, hsem, msem, lsem, gsend, grecv, zsend, zrecv, fsend, frecv, xsend, xrecv,
 ):
     r = lax.axis_index("row")
     c = lax.axis_index("col")
@@ -58,6 +58,12 @@
         return total
 
     peers = [flip(d) for d in range(1, C)][::-1]
+    H = C // 2
+    def slot(p):
+        return (p % 2) * H + p // 2
+    core, mate = c % 2, flip(1)
+    chips = [flip(d) for d in range(2, C, 2)][::-1]
+    me = slot(c)
 
     def panel_copy(b, i):
         return pltpu.make_async_copy(
@@ -75,12 +81,16 @@
     for i in range(nk):
         trail_copy(i).start()
         panel_copy(1, i).start()
-    for i in range(nk):
-        panel_copy(0, i).start()
-    right_copy.start()
-    for b in (1, 2, 0):
-        for j in range(R):
-            mat_copy(b, j).start()
+    def late0():
+        for i in range(nk):
+            panel_copy(0, i).start()
+        right_copy.start()
+
+    def late1():
+        for b in (1, 2, 0):
+            for j in range(R):
+                mat_copy(b, j).start()
+
 
     barrier = pltpu.get_barrier_semaphore()
     for p in peers:
@@ -88,22 +98,6 @@
     for d in range(1, R):
         pl.semaphore_signal(
             barrier, inc=1, device_id=(lax.rem(r + d, R), c), device_id_type=MESH
-        )
-
-    def part_send(b, n):
-        p = peers[n]
-        return pltpu.make_async_remote_copy(
-            src_ref=sbuf.at[b, p], dst_ref=gbuf.at[b, c],
-            send_sem=gsend.at[b, n], recv_sem=grecv.at[b, c],
-            device_id=(r, p), device_id_type=MESH,
-        )
-
-    def part_recv(b, n):
-        p = peers[n]
-        return pltpu.make_async_remote_copy(
-            src_ref=sbuf.at[b, p], dst_ref=gbuf.at[b, p],
-            send_sem=gsend.at[b, n], recv_sem=grecv.at[b, p],
-            device_id=(r, p), device_id_type=MESH,
         )
 
     def partials(b):
@@ -120,26 +114,55 @@
         sbuf[b] = turned.astype(BF16)
         acc_t[b] = turned
 
+
+    def x_copy(b):
+        return pltpu.make_async_remote_copy(
+            src_ref=sbuf.at[b, pl.ds((1 - core) * H, H)], dst_ref=xbuf.at[b],
+            send_sem=xsend.at[b], recv_sem=xrecv.at[b],
+            device_id=(r, mate), device_id_type=MESH,
+        )
+
+    def y_copy(b, n, dst):
+        p = chips[n]
+        return pltpu.make_async_remote_copy(
+            src_ref=ybuf.at[b, p // 2], dst_ref=gbuf.at[b, dst],
+            send_sem=gsend.at[b, n], recv_sem=grecv.at[b, dst],
+            device_id=(r, p), device_id_type=MESH,
+        )
+
+    def mid(b):
+        x_copy(b).wait_recv()
+        both = acc_t[b, pl.ds(core * H, H)] + xbuf[b].astype(F32)
+        acc_t[b, pl.ds(core * H, H)] = both
+        ybuf[b] = both.astype(BF16)
+        for n in range(H - 1):
+            y_copy(b, n, c).start()
+
+    def first_send(b):
+        x_copy(b).start()
+
     partials(1)
+    late0()
     pl.semaphore_wait(barrier, C - 1 + R - 1)
-    for n in range(C - 1):
-        part_send(1, n).start()
+    first_send(1)
+    mid(1)
     partials(0)
-    for n in range(C - 1):
-        part_send(0, n).start()
+    late1()
+    first_send(0)
     right_copy.wait()
     for b in (1, 0):
         h_t[b] = hbuf[b].astype(F32).T.reshape(C, fs, m)
+    mid(0)
     for b in (1, 2, 0):
         for j in range(R):
             mat_copy(b, j).wait()
 
     def residual(b):
-        total = acc_t[b, c]
-        for n in reversed(range(C - 1)):
-            part_recv(b, n).wait_recv()
-            total = total + gbuf[b, peers[n]].astype(F32)
-        return h_t[b, c] - total
+        total = acc_t[b, me]
+        for n in reversed(range(H - 1)):
+            y_copy(b, n, chips[n]).wait_recv()
+            total = total + gbuf[b, chips[n]].astype(F32)
+        return h_t[b, me] - total
 
     def row_send(phase, j):
         return pltpu.make_async_remote_copy(
@@ -172,7 +195,7 @@
     def sol_send(b, n):
         p = peers[n]
         return pltpu.make_async_remote_copy(
-            src_ref=fbuf.at[b], dst_ref=out.at[b, c],
+            src_ref=fbuf.at[b], dst_ref=out.at[b, me],
             send_sem=fsend.at[b, n], recv_sem=frecv.at[b, c],
             device_id=(r, p), device_id_type=MESH,
         )
@@ -180,13 +203,24 @@
     def sol_recv(b, n):
         p = peers[n]
         return pltpu.make_async_remote_copy(
-            src_ref=fbuf.at[b], dst_ref=out.at[b, p],
+            src_ref=fbuf.at[b], dst_ref=out.at[b, slot(p)],
             send_sem=fsend.at[b, n], recv_sem=frecv.at[b, p],
             device_id=(r, p), device_id_type=MESH,
         )
 
+    def gather_start(b):
+        for n in range(C - 1):
+            sol_send(b, n).start()
+        own_copy(b).start()
+
+    def gather_end(b):
+        own_copy(b).wait()
+        for n in range(C - 1):
+            sol_recv(b, n).wait_recv()
+            sol_send(b, n).wait_send()
+
     def own_copy(b):
-        return pltpu.make_async_copy(fbuf.at[b], out.at[b, c], lsem.at[b])
+        return pltpu.make_async_copy(fbuf.at[b], out.at[b, me], lsem.at[b])
 
     next_sol = triangle(0, 1, residual(1).astype(BF16))
 
@@ -200,9 +234,7 @@
         def _():
             row_send(1, r + d).start()
     fbuf[1] = next_sol
-    for n in range(C - 1):
-        sol_send(1, n).start()
-    own_copy(1).start()
+    gather_start(1)
 
     zacc[...] = residual(0)
     for j in reversed(range(R)):
@@ -213,18 +245,14 @@
 
     first_sol = triangle(2, 0, zacc[...].astype(BF16))
     fbuf[0] = first_sol
-    for n in range(C - 1):
-        sol_send(0, n).start()
-    own_copy(0).start()
-
+    gather_start(0)
+
+    gather_end(1)
+    gather_end(0)
     for b in (1, 0):
-        own_copy(b).wait()
-        for n in range(C - 1):
-            sol_recv(b, n).wait_recv()
-    for b in (1, 0):
-        for n in range(C - 1):
-            part_send(b, n).wait_send()
-            sol_send(b, n).wait_send()
+        x_copy(b).wait_send()
+        for n in range(H - 1):
+            y_copy(b, n, c).wait_send()
     for phase in range(3):
         for d in range(1, R):
             @pl.when(r - d >= 0)
@@ -246,7 +274,7 @@
     DMA = pltpu.SemaphoreType.DMA
     out = pl.pallas_call(
         functools.partial(kernel, R, C, nk),
-        out_shape=jax.ShapeDtypeStruct((2, C, fs, m), BF16),
+        out_shape=pltpu.VMEM((2, C, fs, m), BF16),
         in_specs=[any_spec] * 5,
         out_specs=any_spec,
         scratch_shapes=[
@@ -262,17 +290,21 @@
             pltpu.VMEM((3, R, fs, m), BF16),
             pltpu.VMEM((fs, m), F32),
             pltpu.VMEM((2, fs, m), BF16),
+            pltpu.VMEM((2, C // 2, fs, m), BF16),
+            pltpu.VMEM((2, C // 2, fs, m), BF16),
             DMA((2, nk)),
             DMA((nk,)),
             DMA,
             DMA((3, R)),
             DMA((2,)),
-            DMA((2, C - 1)),
+            DMA((2, C // 2)),
             DMA((2, C)),
             DMA((3, R)),
             DMA((3, R)),
             DMA((2, C - 1)),
             DMA((2, C)),
+            DMA((2,)),
+            DMA((2,)),
         ],
         compiler_params=pltpu.CompilerParams(collective_id=0, has_side_effects=True),
     )(factor_panel, solved_trail, right_sides, diag_inverse, coupling)
@@ -286,7 +318,7 @@
         _, m, k = factor_panel.shape
         frames = solved_trail.shape[1]
         fits = (
-            C & (C - 1) == 0 and frames % (16 * C) == 0 and m % 128 == 0
+            C > 2 and C & (C - 1) == 0 and frames % (16 * C) == 0 and m % 128 == 0
             and frames % 128 == 0 and k % 512 == 0
         )
         args = (factor_panel, solved_trail, right_sides, diag_inverse, coupling)

time: 35.7 us -> 32.2 us (0.902)
  Pallas kernels: 33.4 us -> 31 us
  local copies, waits for them, and re-layouts: 2.12 us -> 1.07 us
    pallas_call x1, Pallas kernels: 33.4 us -> 31 us  [fused_shards(): pl.pallas_call(functools.partial(kernel, R, C, nk), out_shape=pltpu.VMEM(...]
    reshape x1, local copies, waits for them, and re-layouts: 2.12 us -> 1.07 us  [fused_shards(): return jnp.swapaxes(out.reshape(2, frames, m), 1, 2)]
where the time goes in v2:
time: 32.2 us; the launch traced here: 32 us
  Pallas kernels  31 us (96%)
  local copies, waits for them, and re-layouts  1.07 us (3%)
    pallas_call x1, Pallas kernels, fused_shards(): pl.pallas_call(functools.partial(kernel, R, C, nk), out_shape=pltpu.VMEM(...  31 us
    reshape x1, local copies, waits for them, and re-layouts, fused_shards(): return jnp.swapaxes(out.reshape(2, frames, m), 1, 2)  1.07 us

profile of v2, /device:TPU:0, one launch (start us, length us, event | category | flops | bytes accessed | tf_op | source)
XLA Modules:
  0.0 32.0 jit_solution(17608613480533110930)
XLA Ops:
  0.0 31.0 %shard_map.55 = bf16[2,8,48,384]{3,2,1,0:T(8,128)(2,1)S(1)} custom-call(bf16[2,384,3072]{2,1,0:T(8,128)(2,1)} %panel.1, bf16[3072,384]{1,0:T(8,128)(2,1)} %trail.1, bf16[2,384,384]{2,1,0:T(8,128)(2,1)} %right.1, bf16[2,384,1536]{2,1,0:T(8,128)(2,1)} %diag.1, bf16[384,1536]{1,0:T(8,128)(2,1)} %coup.1), custom_call_target="tpu_custom_call" | custom-call | tf_op jit(solution)/shard_map/pallas_call | solution.py:275
  31.0 1.1 %copy.6 = bf16[2,384,384]{1,2,0:T(8,128)(2,1)} copy(bf16[2,384,384]{2,1,0:T(8,128)(2,1)S(1)} %bitcast.2) | data formatting | bytes 1179648 | tf_op jit(solution)/shard_map/reshape | solution.py:311

commit v3 on v2

--- a/solution.py
+++ b/solution.py
@@ -40,7 +40,7 @@
     R, C, nk,
     panel, trail, right, diag, coup, out,
     pbuf, tbuf, hbuf, mbuf, acc, acc_t, h_t, sbuf, gbuf, zbuf, zacc, fbuf, xbuf, ybuf,
-    psem, tsem, hsem, msem, lsem, gsend, grecv, zsend, zrecv, fsend, frecv, xsend, xrecv,
+    psem, tsem, hsem, msem, lsem, gsend, grecv, zsend, zrecv, fsend, frecv, xsend, xrecv, vsend, vrecv,
 ):
     r = lax.axis_index("row")
     c = lax.axis_index("col")
@@ -150,13 +150,7 @@
     late1()
     first_send(0)
     right_copy.wait()
-    for b in (1, 0):
-        h_t[b] = hbuf[b].astype(F32).T.reshape(C, fs, m)
-    mid(0)
-    for b in (1, 2, 0):
-        for j in range(R):
-            mat_copy(b, j).wait()
-
+    h_t[1] = hbuf[1].astype(F32).T.reshape(C, fs, m)
     def residual(b):
         total = acc_t[b, me]
         for n in reversed(range(H - 1)):
@@ -184,6 +178,11 @@
             @pl.when(r - d >= 0)
             def _():
                 row_send(phase, r - d).start()
+        if phase == 0:
+            mid(0)
+            h_t[0] = hbuf[0].astype(F32).T.reshape(C, fs, m)
+        for j in range(R):
+            mat_copy(b, j).wait()
         zacc[...] = dot_t(zbuf[phase, r], mbuf[b, r])
         for d in range(1, R):
             @pl.when(r + d < R)
@@ -208,16 +207,43 @@
             device_id=(r, p), device_id_type=MESH,
         )
 
+    relayed = [0]
+    skip = [chips[n] + 1 - 2 * core for n in relayed]
+    def dnum(n):
+        return C - 1 - n
+    rel_d = [C - 2 - 2 * n for n in relayed]
+    direct = [n for n in range(C - 1) if not (dnum(n) % 2 == 1 and dnum(n) - 1 in rel_d)]
+    if relayed:
+        direct = [n for n in direct if dnum(n) in rel_d] + [n for n in direct if dnum(n) not in rel_d]
+
+    def relay(b, n, p):
+        return pltpu.make_async_remote_copy(
+            src_ref=out.at[b, slot(p)], dst_ref=out.at[b, slot(p)],
+            send_sem=vsend.at[b, n], recv_sem=vrecv.at[b, n],
+            device_id=(r, mate), device_id_type=MESH,
+        )
+
     def gather_start(b):
-        for n in range(C - 1):
+        for n in direct:
             sol_send(b, n).start()
         own_copy(b).start()
 
+    def gather_mid(b):
+        for n in relayed:
+            sol_recv(b, C - 1 - rel_d[n]).wait_recv()
+            relay(b, n, chips[n]).start()
+
     def gather_end(b):
         own_copy(b).wait()
-        for n in range(C - 1):
-            sol_recv(b, n).wait_recv()
+        for n in direct:
+            if dnum(n) not in rel_d:
+                sol_recv(b, n).wait_recv()
+        for n in relayed:
+            relay(b, n, flip(rel_d[n] + 1)).wait_recv()
+        for n in direct:
             sol_send(b, n).wait_send()
+        for n in relayed:
+            relay(b, n, chips[n]).wait_send()
 
     def own_copy(b):
         return pltpu.make_async_copy(fbuf.at[b], out.at[b, me], lsem.at[b])
@@ -237,16 +263,20 @@
     gather_start(1)
 
     zacc[...] = residual(0)
+    for j in range(R):
+        mat_copy(2, j).wait()
     for j in reversed(range(R)):
         @pl.when(r != j)
         def _():
             row_recv(1, j).wait_recv()
         zacc[...] -= dot_t(zbuf[1, j], mbuf[2, j])
 
+    gather_mid(1)
     first_sol = triangle(2, 0, zacc[...].astype(BF16))
     fbuf[0] = first_sol
     gather_start(0)
 
+    gather_mid(0)
     gather_end(1)
     gather_end(0)
     for b in (1, 0):
@@ -305,6 +335,8 @@
             DMA((2, C)),
             DMA((2,)),
             DMA((2,)),
+            DMA((2, C // 2)),
+            DMA((2, C // 2)),
         ],
         compiler_params=pltpu.CompilerParams(collective_id=0, has_side_effects=True),
     )(factor_panel, solved_trail, right_sides, diag_inverse, coupling)

time: 32.2 us -> 32 us (level)
  no operation moved by 1% of the time
where the time goes in v3:
time: 32 us; the launch traced here: 31.9 us
  Pallas kernels  30.8 us (96%)
  local copies, waits for them, and re-layouts  1.07 us (3%)
    pallas_call x1, Pallas kernels, fused_shards(): pl.pallas_call(functools.partial(kernel, R, C, nk), out_shape=pltpu.VMEM(...  30.8 us
    reshape x1, local copies, waits for them, and re-layouts, fused_shards(): return jnp.swapaxes(out.reshape(2, frames, m), 1, 2)  1.07 us

profile of v3, /device:TPU:0, one launch (start us, length us, event | category | flops | bytes accessed | tf_op | source)
XLA Modules:
  0.0 31.9 jit_solution(17846896276158688009)
XLA Ops:
  0.0 30.8 %shard_map.55 = bf16[2,8,48,384]{3,2,1,0:T(8,128)(2,1)S(1)} custom-call(bf16[2,384,3072]{2,1,0:T(8,128)(2,1)} %panel.1, bf16[3072,384]{1,0:T(8,128)(2,1)} %trail.1, bf16[2,384,384]{2,1,0:T(8,128)(2,1)} %right.1, bf16[2,384,1536]{2,1,0:T(8,128)(2,1)} %diag.1, bf16[384,1536]{1,0:T(8,128)(2,1)} %coup.1), custom_call_target="tpu_custom_call" | custom-call | tf_op jit(solution)/shard_map/pallas_call | solution.py:305
  30.8 1.1 %copy.6 = bf16[2,384,384]{1,2,0:T(8,128)(2,1)} copy(bf16[2,384,384]{2,1,0:T(8,128)(2,1)S(1)} %bitcast.2) | data formatting | bytes 1179648 | tf_op jit(solution)/shard_map/reshape | solution.py:343
